TPU v7x, 32 devices: a whole 2x2x4 slice. The times are simulated.
32 devices in a mesh: tm: 8 (over z, core), space: 4 (over y, x).
Axes of the slice: x: 2, y: 2, z: 4, core: 2. Of those that a mesh axis runs over, the one named last changes fastest.
Arguments:
- initial_temp: float32 [64, 32, 256], P('space'), may hold values from -6 to 6
- region_labels: int32 [16, 8, 64], P('space'), may hold values from 0 to 5
- region_rate: float32 [6], replicated, may hold values from 0.5 to 8
- heat_rate: float32 [8, 6], replicated, may hold values from 0.1 to 2
Outputs:
- slice_end: float32 [8, 64, 32, 256], P('tm', 'space')
All inputs are finite; a program needn't handle non-finite values.
Results may differ from a plain program's by a relative error of at most 0.0001.
Values sent between devices are 32-bit elements; how exact they have to be, the bound alone decides.
A program may use at most 128 MiB of HBM per device.

v0:
```python
import jax
import jax.numpy as jnp
from jax import lax
from jax.sharding import PartitionSpec as P

FINE_STEPS = 2
SWEEPS = 8
C_SWEEPS = 4
PARA_ITERS = 2


def with_halo(array, sides, width):
    for axis, dim in sides:
        peers, length = (lax.axis_size(axis), array.shape[dim])
        up = [(i, (i + 1) % peers) for i in range(peers - 1)]
        down = [(j, i) for i, j in up]
        last = lax.slice_in_dim(array, length - width, length, axis=dim)
        initial = lax.slice_in_dim(array, 0, width, axis=dim)
        before = lax.ppermute(last, axis, up)
        after = lax.ppermute(initial, axis, down)
        array = jnp.concatenate([before, array, after], axis=dim)
    return array


def shifted(array, axis, by):
    peers = lax.axis_size(axis)
    pairs = [(i, i + by) for i in range(peers) if 0 <= i + by < peers]
    return lax.ppermute(array, axis, pairs)


def neighbours(field):
    padded = jnp.pad(field, 1)
    total = padded[2:, 1:-1, 1:-1] + padded[:-2, 1:-1, 1:-1]
    total = total + padded[1:-1, 2:, 1:-1] + padded[1:-1, :-2, 1:-1]
    total = total + padded[1:-1, 1:-1, 2:] + padded[1:-1, 1:-1, :-2]
    return total


def expand(block):
    sx, sy, sz = block.shape
    wide = jnp.broadcast_to(block[:, None, :, None, :, None], (sx, 4, sy, 4, sz, 4))
    return wide.reshape((4 * sx, 4 * sy, 4 * sz))


def restrict(field):
    sx, sy, sz = field.shape
    split = field.reshape((sx // 4, 4, sy // 4, 4, sz // 4, 4))
    return jnp.mean(split, axis=(1, 3, 5))


def lookup(labels, table):
    total = jnp.zeros(labels.shape, jnp.float32)
    for region in range(table.shape[0]):
        total = total + jnp.where(labels == region, table[region], jnp.float32(0.0))
    return total


def on_device(initial_temp, region_labels, region_rate, heat_rate):
    slice_index = lax.axis_index("tm")
    slice_count = lax.axis_size("tm")
    heat_row = lax.dynamic_index_in_dim(heat_rate, slice_index, 0, keepdims=False)
    rate_block = lookup(region_labels, region_rate)
    rate_fine = expand(rate_block)
    inv_fine = 1.0 / (1.0 + 6.0 * rate_fine)
    weight_fine = rate_fine * inv_fine
    source_fine = expand(lookup(region_labels, heat_row))
    rim_width = 4
    fine_coeffs = with_halo(
        jnp.stack([inv_fine, weight_fine, source_fine]), (("space", 1),), rim_width
    )

    def fine_halo(field):
        return with_halo(field, (("space", 0),), rim_width)

    rate_coarse = FINE_STEPS * rate_block / 16.0
    inv_coarse = 1.0 / (1.0 + 6.0 * rate_coarse)
    weight_coarse = rate_coarse * inv_coarse
    source_coarse = FINE_STEPS * lookup(region_labels, heat_row)
    coarse_coeffs = with_halo(
        jnp.stack([inv_coarse, weight_coarse, source_coarse]), (("space", 1),), C_SWEEPS
    )
    start = restrict(initial_temp)

    def coarse_step(coarse):
        field_ext = with_halo(coarse, (("space", 0),), C_SWEEPS)
        scaled = (field_ext + coarse_coeffs[2]) * coarse_coeffs[0]
        for sweep_index in range(C_SWEEPS):
            field_ext = scaled + coarse_coeffs[1] * neighbours(field_ext)
        return field_ext[C_SWEEPS:-C_SWEEPS]

    def run_chain(delta):
        offset = jnp.zeros_like(start) if delta is None else delta

        def turn(turn_index, incoming):
            moved = shifted(coarse_step(incoming) + offset, "tm", 1)
            return jnp.where(slice_index == 0, start, moved)

        arrived = lax.fori_loop(0, slice_count - 1, turn, start)
        return (arrived, coarse_step(arrived))

    own_start, previous_end = run_chain(None)
    state = jnp.where(slice_index == 0, initial_temp, expand(own_start))
    result = state
    for iteration in range(PARA_ITERS):
        fine_state = state
        for fine_step in range(FINE_STEPS):
            fine_field_ext = fine_halo(fine_state)
            fine_scaled = (fine_field_ext + fine_coeffs[2]) * fine_coeffs[0]
            for block_index in range(SWEEPS // rim_width):
                if block_index > 0:
                    fine_field_ext = fine_halo(fine_state)
                for fine_sweep_index in range(rim_width):
                    fine_field_ext = fine_scaled + fine_coeffs[1] * neighbours(fine_field_ext)
                fine_state = fine_field_ext[rim_width:-rim_width]
        delta = restrict(fine_state) - previous_end
        own_start, own_end = run_chain(delta)
        correction = own_end - previous_end
        previous_end = own_end
        if iteration + 1 < PARA_ITERS:
            moved = shifted(fine_state + expand(correction), "tm", 1)
            state = jnp.where(slice_index == 0, initial_temp, moved)
        else:
            result = fine_state + expand(correction)
    return result[None]


def solution(mesh):
    return jax.shard_map(
        on_device,
        mesh=mesh,
        in_specs=(P("space", None, None), P("space", None, None), P(), P()),
        out_specs=P("tm", "space", None, None),
        check_vma=False,
    )
```

profile of v0, /device:TPU:27, one launch (start us, length us, event | category | flops | bytes accessed | tf_op | source)
XLA Modules:
  0.0 652.3 jit_solution(1840460029188388304)
XLA Ops:
  2.2 4.6 fusion.337
  6.8 3.7 multiply_bitcast_fusion
  12.7 4.0 collective-permute-start.9
  16.8 8.0 %broadcast_in_dim.112 = f32[4,4,8,4,64,4]{5,4,3,2,1,0:T(8,128)} broadcast(f32[4,8,64]{2,1,0:T(8,128)S(1)} %get-tuple-element.300), dimensions={0,2,4} | broadcast | bytes 532480 | tf_op jit(solution)/shard_map/broadcast_in_dim | solution.py:41
  24.8 15.0 %stack_reshape.3 = f32[1,16,32,256]{3,2,1,0:T(8,128)S(1)} reshape(f32[4,4,8,4,64,4]{5,4,3,2,1,0:T(8,128)} %broadcast_in_dim.112) | data formatting | bytes 1048576 | tf_op jit(solution)/shard_map/stack;reshape | solution.py:69
  39.8 8.0 %broadcast_in_dim.111 = f32[4,4,8,4,64,4]{5,4,3,2,1,0:T(8,128)} broadcast(f32[4,8,64]{2,1,0:T(8,128)S(1)} %get-tuple-element.292), dimensions={0,2,4} | broadcast | bytes 532480 | tf_op jit(solution)/shard_map/broadcast_in_dim | solution.py:41
  47.8 15.0 %reshape.69 = f32[1,16,32,256]{3,2,1,0:T(8,128)S(1)} reshape(f32[4,4,8,4,64,4]{5,4,3,2,1,0:T(8,128)} %broadcast_in_dim.111) | data formatting | bytes 1048576 | tf_op jit(solution)/shard_map/reshape | solution.py:42
  68.4 18.6 %reshape.67 = f32[4,4,8,4,64,4]{5,4,3,2,1,0:T(8,128)} reshape(f32[16,32,256]{2,1,0:T(8,128)S(1)} %copy-done.2) | data formatting | bytes 1048576 | tf_op jit(solution)/shard_map/reshape | solution.py:47
  87.0 7.0 %reduce_sum.27 = f32[4,8,64]{2,1,0:T(8,128)S(1)} reduce(f32[4,4,8,4,64,4]{5,4,3,2,1,0:T(8,128)} %reshape.67, f32[]{:T(128)} %constant.79.clone.1), dimensions={1,3,5}, to_apply=%region_0.1 | reduce | flops 129024 | bytes 532484 | tf_op jit(solution)/shard_map/reduce_sum | solution.py:48
  95.6 98.3 %while.36 = (s32[]{:T(128)}, f32[4,8,64]{2,1,0:T(8,128)S(1)}, pred[]{:T(512)}, f32[3,12,8,64]{3,2,1,0:T(8,128)S(1)}, f32[4,8,64]{2,1,0:T(8,128)S(1)}, /*index=5*/s32[]{:T(128)}) while((s32[]{:T(128)}, f32[4,8,64]{2,1,0:T(8,128)S(1)}, pred[]{:T(512)}, f32[3,12,8,64]{3,2,1,0:T(8,128)S(1)}, f32[4,8,64]{2,1,0:T(8,128)S(1)}, ...), condition=%wide.region_2.3_spmd, body=%wide.region_1.2_spmd.sunk | while | flops 161794 | bytes 819390 | solution.py:98
  105.8 4.5 collective-permute-done.2
  119.4 4.9 collective-permute-done.2
  133.3 4.9 collective-permute-done.2
  147.2 4.9 collective-permute-done.2
  161.2 4.9 collective-permute-done.2
  175.1 4.9 collective-permute-done.2
  189.0 4.9 collective-permute-done.2
  195.8 3.8 collective-permute-start.22
  199.7 8.0 %broadcast_in_dim.110 = f32[4,4,8,4,64,4]{5,4,3,2,1,0:T(8,128)} broadcast(f32[4,8,64]{2,1,0:T(8,128)S(1)} %get-tuple-element.230), dimensions={0,2,4} | broadcast | bytes 532480 | tf_op jit(solution)/shard_map/broadcast_in_dim | solution.py:41
  207.7 15.0 %reshape.68 = f32[16,32,256]{2,1,0:T(8,128)S(1)} reshape(f32[4,4,8,4,64,4]{5,4,3,2,1,0:T(8,128)} %broadcast_in_dim.110) | data formatting | bytes 1048576 | tf_op jit(solution)/shard_map/reshape | solution.py:42
  229.2 3.8 collective-permute-done.12
  254.8 4.0 collective-permute-done.18
  266.7 4.0 collective-permute-done.20
  275.1 19.4 %reshape.70 = f32[4,4,8,4,64,4]{5,4,3,2,1,0:T(8,128)} reshape(f32[16,32,256]{2,1,0:T(8,128)} %slice_add_fusion.40) | data formatting | bytes 1048576 | tf_op jit(solution)/shard_map/reshape | solution.py:47
  294.6 7.1 %reduce_sum.28 = f32[4,8,64]{2,1,0:T(8,128)S(1)} reduce(f32[4,4,8,4,64,4]{5,4,3,2,1,0:T(8,128)} %reshape.70, f32[]{:T(128)} %constant.79.clone.1), dimensions={1,3,5}, to_apply=%region_3.4 | reduce | flops 129024 | bytes 532484 | tf_op jit(solution)/shard_map/reduce_sum | solution.py:48
  301.6 99.6 %while.37 = (s32[]{:T(128)}, f32[4,8,64]{2,1,0:T(8,128)S(1)}, pred[]{:T(512)}, f32[3,12,8,64]{3,2,1,0:T(8,128)S(1)}, f32[4,8,64]{2,1,0:T(8,128)S(1)}, /*index=5*/f32[4,8,64]{2,1,0:T(8,128)S(1)}, s32[]{:T(128)}) while((s32[]{:T(128)}, f32[4,8,64]{2,1,0:T(8,128)S(1)}, pred[]{:T(512)}, f32[3,12,8,64]{3,2,1,0:T(8,128)S(1)}, ...), condition=%wide.region_5.6_spmd, body=%wide.region_4.5_spmd.sunk | while | flops 163842 | bytes 827590 | solution.py:98
  310.7 7.0 %collective-permute-done.5 = f32[4,8,64]{2,1,0:T(8,128)S(1)} collective-permute-done((f32[4,8,64]{2,1,0:T(8,128)S(1)}, f32[4,8,64]{2,1,0:T(8,128)S(1)}, u32[]{:S(2)}, u32[]{:S(2)}) %collective-permute-start.5) | collective-permute-done | bytes 8224 | tf_op jit(solution)/shard_map/while/body/eval_jaxpr/ppermute | solution.py:28
  326.7 4.9 collective-permute-done.5
  340.6 4.9 collective-permute-done.5
  354.6 4.9 collective-permute-done.5
  368.5 4.9 collective-permute-done.5
  382.4 4.9 collective-permute-done.5
  396.4 4.9 collective-permute-done.5
  409.0 8.0 %broadcast_in_dim.113 = f32[4,4,8,4,64,4]{5,4,3,2,1,0:T(8,128)} broadcast(f32[4,8,64]{2,1,0:T(8,128)S(1)} %get-tuple-element.279), dimensions={0,2,4} | broadcast | bytes 532480 | tf_op jit(solution)/shard_map/broadcast_in_dim | solution.py:41
  417.0 15.6 %reshape.71 = f32[16,32,256]{2,1,0:T(8,128)} reshape(f32[4,4,8,4,64,4]{5,4,3,2,1,0:T(8,128)} %broadcast_in_dim.113) | data formatting | bytes 1048576 | tf_op jit(solution)/shard_map/reshape | solution.py:42
  435.2 5.6 collective-permute-done.25
  487.6 18.6 %reshape.72 = f32[4,4,8,4,64,4]{5,4,3,2,1,0:T(8,128)} reshape(f32[16,32,256]{2,1,0:T(8,128)S(1)} %slice_add_fusion.35) | data formatting | bytes 1048576 | tf_op jit(solution)/shard_map/reshape | solution.py:47
  506.3 7.0 %reduce_sum.29 = f32[4,8,64]{2,1,0:T(8,128)S(1)} reduce(f32[4,4,8,4,64,4]{5,4,3,2,1,0:T(8,128)} %reshape.72, f32[]{:T(128)} %constant.79.clone.1), dimensions={1,3,5}, to_apply=%region_6.7 | reduce | flops 129024 | bytes 532484 | tf_op jit(solution)/shard_map/reduce_sum | solution.py:48
  513.3 106.9 %while.38 = (s32[]{:T(128)}, f32[4,8,64]{2,1,0:T(8,128)S(1)}, pred[]{:T(512)}, f32[3,12,8,64]{3,2,1,0:T(8,128)S(1)}, f32[4,8,64]{2,1,0:T(8,128)S(1)}, /*index=5*/f32[4,8,64]{2,1,0:T(8,128)S(1)}, s32[]{:T(128)}) while((s32[]{:T(128)}, f32[4,8,64]{2,1,0:T(8,128)S(1)}, pred[]{:T(512)}, f32[3,12,8,64]{3,2,1,0:T(8,128)S(1)}, ...), condition=%wide.region_8.9_spmd, body=%wide.region_7.8_spmd.sunk | while | flops 163842 | bytes 827590 | solution.py:98
  522.4 14.2 %collective-permute-done.8 = f32[4,8,64]{2,1,0:T(8,128)S(1)} collective-permute-done((f32[4,8,64]{2,1,0:T(8,128)S(1)}, f32[4,8,64]{2,1,0:T(8,128)S(1)}, u32[]{:S(2)}, u32[]{:S(2)}) %collective-permute-start.8) | collective-permute-done | bytes 8224 | tf_op jit(solution)/shard_map/while/body/eval_jaxpr/ppermute | solution.py:28
  545.6 4.9 collective-permute-done.8
  559.5 4.9 collective-permute-done.8
  573.5 4.9 collective-permute-done.8
  587.4 4.9 collective-permute-done.8
  601.3 4.9 collective-permute-done.8
  615.3 4.9 collective-permute-done.8
  627.9 8.0 %broadcast_in_dim.114 = f32[4,4,8,4,64,4]{5,4,3,2,1,0:T(8,128)} broadcast(f32[4,8,64]{2,1,0:T(8,128)S(1)} %fusion.333), dimensions={0,2,4} | broadcast | bytes 532480 | tf_op jit(solution)/shard_map/broadcast_in_dim | solution.py:41
  635.9 15.0 %reshape.73 = f32[16,32,256]{2,1,0:T(8,128)S(1)} reshape(f32[4,4,8,4,64,4]{5,4,3,2,1,0:T(8,128)} %broadcast_in_dim.114) | data formatting | bytes 1048576 | tf_op jit(solution)/shard_map/reshape | solution.py:42
  (489 shorter events, 307.8 us)
Async XLA Ops:
  10.6 83.6 %collective-permute-start.10 = (f32[3,4,8,64]{3,2,1,0:T(8,128)S(1)}, f32[3,4,8,64]{3,2,1,0:T(8,128)S(1)}, u32[]{:S(2)}, u32[]{:S(2)}) collective-permute-start(f32[3,4,8,64]{3,2,1,0:T(8,128)S(1)} %pad_maximum_fusion.9), channel_id=1, source_target_pairs={{1,0},{2,1},{3,2},{5,4},{6,5},{7,6},{9,8},{10,9},{11,10},{13,12},{... | collective-permute-start | bytes 73736 | tf_op jit(solution)/shard_map/ppermute | solution.py:20
  12.7 82.0 %collective-permute-start.9 = (f32[3,4,8,64]{3,2,1,0:T(8,128)S(1)}, f32[3,4,8,64]{3,2,1,0:T(8,128)}, u32[]{:S(2)}, u32[]{:S(2)}) collective-permute-start(f32[3,4,8,64]{3,2,1,0:T(8,128)S(1)} %pad_maximum_fusion.9), channel_id=1, source_target_pairs={{0,1},{1,2},{2,3},{4,5},{5,6},{6,7},{8,9},{9,10},{10,11},{12,13},{... | collective-permute-start | bytes 73736 | tf_op jit(solution)/shard_map/ppermute | solution.py:19
  63.1 170.0 %collective-permute-start.13 = (f32[3,4,32,256]{3,2,1,0:T(8,128)S(1)}, f32[3,4,32,256]{3,2,1,0:T(8,128)S(1)}, u32[]{:S(2)}, u32[]{:S(2)}) collective-permute-start(f32[3,4,32,256]{3,2,1,0:T(8,128)S(1)} %get-tuple-element.316), channel_id=1, source_target_pairs={{0,1},{1,2},{2,3},{4,5},{5,6},{6,7},{8,9},{9,10},{10,11},{12,13},{... | collective-permute-start | bytes 1179656 | tf_op jit(solution)/shard_map/ppermute | solution.py:19
  65.3 167.8 %collective-permute-start.14 = (f32[3,4,32,256]{3,2,1,0:T(8,128)S(1)}, f32[3,4,32,256]{3,2,1,0:T(8,128)}, u32[]{:S(2)}, u32[]{:S(2)}) collective-permute-start(f32[3,4,32,256]{3,2,1,0:T(8,128)S(1)} %get-tuple-element.317), channel_id=1, source_target_pairs={{1,0},{2,1},{3,2},{5,4},{6,5},{7,6},{9,8},{10,9},{11,10},{13,12},{... | collective-permute-start | bytes 1179656 | tf_op jit(solution)/shard_map/ppermute | solution.py:20
  104.5 5.8 collective-permute-start.2
  118.1 6.2 collective-permute-start.2
  132.0 6.2 collective-permute-start.2
  145.9 6.2 collective-permute-start.2
  159.9 6.2 collective-permute-start.2
  168.0 5.4 collective-permute-start.1
  173.8 6.2 collective-permute-start.2
  181.9 5.4 collective-permute-start.1
  187.7 6.2 collective-permute-start.2
  193.9 32.4 %collective-permute-start.21 = (f32[4,8,64]{2,1,0:T(8,128)S(1)}, f32[4,8,64]{2,1,0:T(8,128)S(1)}, u32[]{:S(2)}, u32[]{:S(2)}) collective-permute-start(f32[4,8,64]{2,1,0:T(8,128)S(1)} %get-tuple-element.230), channel_id=1, source_target_pairs={{0,1},{1,2},{2,3},{4,5},{5,6},{6,7},{8,9},{9,10},{10,11},{12,13},{... | collective-permute-start | bytes 24584 | tf_op jit(solution)/shard_map/ppermute | solution.py:19
  195.8 33.0 %collective-permute-start.22 = (f32[4,8,64]{2,1,0:T(8,128)S(1)}, f32[4,8,64]{2,1,0:T(8,128)S(1)}, u32[]{:S(2)}, u32[]{:S(2)}) collective-permute-start(f32[4,8,64]{2,1,0:T(8,128)S(1)} %get-tuple-element.230), channel_id=1, source_target_pairs={{1,0},{2,1},{3,2},{5,4},{6,5},{7,6},{9,8},{10,9},{11,10},{13,12},{... | collective-permute-start | bytes 24584 | tf_op jit(solution)/shard_map/ppermute | solution.py:20
  223.5 5.7 collective-permute-start.11
  226.3 6.7 %collective-permute-start.12 = (f32[4,32,256]{2,1,0:T(8,128)S(1)}, f32[4,32,256]{2,1,0:T(8,128)S(1)}, u32[]{:S(2)}, u32[]{:S(2)}) collective-permute-start(f32[4,32,256]{2,1,0:T(8,128)S(1)} %get-tuple-element.345), channel_id=1, source_target_pairs={{1,0},{2,1},{3,2},{5,4},{6,5},{7,6},{9,8},{10,9},{11,10},{13,12},{... | collective-permute-start | bytes 393224 | tf_op jit(solution)/shard_map/ppermute | solution.py:20
  236.5 5.7 collective-permute-start.15
  238.4 7.4 %collective-permute-start.16 = (f32[4,32,256]{2,1,0:T(8,128)S(1)}, f32[4,32,256]{2,1,0:T(8,128)S(1)}, u32[]{:S(2)}, u32[]{:S(2)}) collective-permute-start(f32[4,32,256]{2,1,0:T(8,128)S(1)} %get-tuple-element.339), channel_id=1, source_target_pairs={{1,0},{2,1},{3,2},{5,4},{6,5},{7,6},{9,8},{10,9},{11,10},{13,12},{... | collective-permute-start | bytes 393224 | tf_op jit(solution)/shard_map/ppermute | solution.py:20
  249.1 5.7 collective-permute-start.17
  251.0 7.8 %collective-permute-start.18 = (f32[4,32,256]{2,1,0:T(8,128)S(1)}, f32[4,32,256]{2,1,0:T(8,128)S(1)}, u32[]{:S(2)}, u32[]{:S(2)}) collective-permute-start(f32[4,32,256]{2,1,0:T(8,128)S(1)} %get-tuple-element.337), channel_id=1, source_target_pairs={{1,0},{2,1},{3,2},{5,4},{6,5},{7,6},{9,8},{10,9},{11,10},{13,12},{... | collective-permute-start | bytes 393224 | tf_op jit(solution)/shard_map/ppermute | solution.py:20
  261.0 5.7 collective-permute-start.19
  262.9 7.8 %collective-permute-start.20 = (f32[4,32,256]{2,1,0:T(8,128)S(1)}, f32[4,32,256]{2,1,0:T(8,128)S(1)}, u32[]{:S(2)}, u32[]{:S(2)}) collective-permute-start(f32[4,32,256]{2,1,0:T(8,128)S(1)} %get-tuple-element.335), channel_id=1, source_target_pairs={{1,0},{2,1},{3,2},{5,4},{6,5},{7,6},{9,8},{10,9},{11,10},{13,12},{... | collective-permute-start | bytes 393224 | tf_op jit(solution)/shard_map/ppermute | solution.py:20
  303.6 5.4 collective-permute-start.4
  309.4 8.3 %collective-permute-start.5 = (f32[4,8,64]{2,1,0:T(8,128)S(1)}, f32[4,8,64]{2,1,0:T(8,128)S(1)}, u32[]{:S(2)}, u32[]{:S(2)}) collective-permute-start(f32[4,8,64]{2,1,0:T(8,128)S(1)} %fusion.372), channel_id=1, source_target_pairs={{0,4},{4,8},{8,12},{12,16},{16,20},{20,24},{24,28},{1,5},{5,9},{9,... | collective-permute-start | bytes 24584 | tf_op jit(solution)/shard_map/while/body/eval_jaxpr/ppermute | solution.py:28
  325.4 6.2 collective-permute-start.5
  333.5 5.4 collective-permute-start.4
  339.3 6.2 collective-permute-start.5
  353.3 6.2 collective-permute-start.5
  367.2 6.2 collective-permute-start.5
  381.1 6.2 collective-permute-start.5
  395.1 6.2 collective-permute-start.5
  433.9 6.9 %collective-permute-start.25 = (f32[16,32,256]{2,1,0:T(8,128)S(1)}, f32[16,32,256]{2,1,0:T(8,128)S(1)}, u32[]{:S(2)}, u32[]{:S(2)}) collective-permute-start(f32[16,32,256]{2,1,0:T(8,128)S(1)} %add.1628), channel_id=1, source_target_pairs={{0,4},{4,8},{8,12},{12,16},{16,20},{20,24},{24,28},{1,5},{5,9},{9,... | collective-permute-start | bytes 1572872 | tf_op jit(solution)/shard_map/ppermute | solution.py:28
  441.0 6.0 collective-permute-start.26
  442.9 6.6 %collective-permute-start.27 = (f32[4,32,256]{2,1,0:T(8,128)S(1)}, f32[4,32,256]{2,1,0:T(8,128)S(1)}, u32[]{:S(2)}, u32[]{:S(2)}) collective-permute-start(f32[4,32,256]{2,1,0:T(8,128)S(1)} %get-tuple-element.341), channel_id=1, source_target_pairs={{1,0},{2,1},{3,2},{5,4},{6,5},{7,6},{9,8},{10,9},{11,10},{13,12},{... | collective-permute-start | bytes 393224 | tf_op jit(solution)/shard_map/ppermute | solution.py:20
  451.8 5.7 collective-permute-start.28
  453.7 6.6 %collective-permute-start.29 = (f32[4,32,256]{2,1,0:T(8,128)S(1)}, f32[4,32,256]{2,1,0:T(8,128)S(1)}, u32[]{:S(2)}, u32[]{:S(2)}) collective-permute-start(f32[4,32,256]{2,1,0:T(8,128)S(1)} %get-tuple-element.328), channel_id=1, source_target_pairs={{1,0},{2,1},{3,2},{5,4},{6,5},{7,6},{9,8},{10,9},{11,10},{13,12},{... | collective-permute-start | bytes 393224 | tf_op jit(solution)/shard_map/ppermute | solution.py:20
  463.6 5.8 collective-permute-start.30
  465.5 6.6 %collective-permute-start.31 = (f32[4,32,256]{2,1,0:T(8,128)S(1)}, f32[4,32,256]{2,1,0:T(8,128)S(1)}, u32[]{:S(2)}, u32[]{:S(2)}) collective-permute-start(f32[4,32,256]{2,1,0:T(8,128)S(1)} %get-tuple-element.326), channel_id=1, source_target_pairs={{1,0},{2,1},{3,2},{5,4},{6,5},{7,6},{9,8},{10,9},{11,10},{13,12},{... | collective-permute-start | bytes 393224 | tf_op jit(solution)/shard_map/ppermute | solution.py:20
  474.4 6.2 collective-permute-start.32
  476.4 7.1 %collective-permute-start.33 = (f32[4,32,256]{2,1,0:T(8,128)S(1)}, f32[4,32,256]{2,1,0:T(8,128)S(1)}, u32[]{:S(2)}, u32[]{:S(2)}) collective-permute-start(f32[4,32,256]{2,1,0:T(8,128)S(1)} %get-tuple-element.324), channel_id=1, source_target_pairs={{1,0},{2,1},{3,2},{5,4},{6,5},{7,6},{9,8},{10,9},{11,10},{13,12},{... | collective-permute-start | bytes 393224 | tf_op jit(solution)/shard_map/ppermute | solution.py:20
  521.1 15.5 %collective-permute-start.8 = (f32[4,8,64]{2,1,0:T(8,128)S(1)}, f32[4,8,64]{2,1,0:T(8,128)S(1)}, u32[]{:S(2)}, u32[]{:S(2)}) collective-permute-start(f32[4,8,64]{2,1,0:T(8,128)S(1)} %fusion.377), channel_id=1, source_target_pairs={{0,4},{4,8},{8,12},{12,16},{16,20},{20,24},{24,28},{1,5},{5,9},{9,... | collective-permute-start | bytes 24584 | tf_op jit(solution)/shard_map/while/body/eval_jaxpr/ppermute | solution.py:28
  544.3 6.2 collective-permute-start.8
  558.2 6.2 collective-permute-start.8
  572.2 6.2 collective-permute-start.8
  586.1 6.2 collective-permute-start.8
  600.0 6.2 collective-permute-start.8
  614.0 6.2 collective-permute-start.8
  (55 other events, 365.6 us)
where the time goes:
time: 666 us; the launch traced here: 652 us
  starting transfers between devices  210 us (32%)
  waiting for transfers between devices  195 us (29%)
  local copies, waits for them, and re-layouts  177 us (27%)
  other arithmetic  66.8 us (10%)
    ppermute x22, waiting for transfers between devices, shifted(): return lax.ppermute(array, axis, pairs)  120 us
    ppermute x34, starting transfers between devices, with_halo(): after = lax.ppermute(initial, axis, down)  112 us
    ppermute x34, waiting for transfers between devices, with_halo(): after = lax.ppermute(initial, axis, down)  72.8 us
    ppermute x34, starting transfers between devices, with_halo(): before = lax.ppermute(last, axis, up)  69.5 us
    reshape x4, local copies, waits for them, and re-layouts, expand(): return wide.reshape((4 * sx, 4 * sy, 4 * sz))  60.7 us
    reshape x3, local copies, waits for them, and re-layouts, restrict(): split = field.reshape((sx // 4, 4, sy // 4, 4, sz // 4, 4))  56.7 us
    broadcast_in_dim x5, local copies, waits for them, and re-layouts, expand(): jnp.broadcast_to(block[:, None, :, None, :, None], (sx, 4, sy, 4, sz, 4))  40 us
    ppermute x22, starting transfers between devices, shifted(): return lax.ppermute(array, axis, pairs)  28.4 us
  transfers between devices with their start and end apart: 90, of which 61 were waited for; matrix products, arithmetic and copies ran while one was open for 15% of the time, Pallas kernels for 0%

commit v1 on v0

v1 whole, which is shorter than its diff:
```python
import functools

import jax
import jax.numpy as jnp
from jax import lax
from jax.experimental import pallas as pl
from jax.experimental.pallas import tpu as pltpu
from jax.sharding import PartitionSpec as P

FINE_STEPS = 2
SWEEPS = 8
C_SWEEPS = 4
W1 = FINE_STEPS * SWEEPS
W2 = SWEEPS
F32 = jnp.float32
MESH = pl.DeviceIdType.MESH
HI = lax.Precision.HIGHEST


def dot(a, b):
    return jnp.dot(a, b, precision=HI, preferred_element_type=F32)


def select_matrix(shape, small_axis):
    small = lax.broadcasted_iota(jnp.int32, shape, small_axis)
    large = lax.broadcasted_iota(jnp.int32, shape, 1 - small_axis)
    hit = (large >= 4 * small) & (large < 4 * small + 4)
    return jnp.where(hit, F32(1.0), F32(0.0))


def kernel(
    n_count, s_count,
    init, labels, rates, heat,
    out,
    ag, gag, t0, u, sc, wt, inv, src, fs, fr, mid, kp, es, er, cs, cr, dcur,
    ag_ss, ag_rs, ih_ss, ih_rs, f_ss, f_rs, m_ss, m_rs, e_ss, e_rs, c_ss, c_rs,
):
    n = lax.axis_index("tm")
    s = lax.axis_index("space")
    planes, ny, nz = init.shape
    bx, cy, cz = labels.shape
    cx = bx * s_count
    lanes = ag.shape[-1]
    regions = rates.shape[1]
    pad = W1 // 4
    has_prev, has_next = n > 0, n < n_count - 1
    has_lo, has_hi = s > 0, s < s_count - 1

    barrier = pltpu.get_barrier_semaphore()
    def greet(cond, dev):
        @pl.when(cond)
        def _():
            pl.semaphore_signal(barrier, inc=1, device_id=dev, device_id_type=MESH)
    def one(c):
        return jnp.where(c, 1, 0).astype(jnp.int32)
    for j in range(1, s_count):
        pl.semaphore_signal(
            barrier, inc=1, device_id=(n, lax.rem(s + j, s_count)), device_id_type=MESH)
    partners = s_count - 1
    for cond_n, dn in ((has_prev, -1), (has_next, 1)):
        for cond_s, ds in ((None, 0), (has_lo, -1), (has_hi, 1)):
            cond = cond_n if cond_s is None else cond_n & cond_s
            greet(cond, (n + dn, s + ds))
            partners = partners + one(cond)
    pl.semaphore_wait(barrier, partners)

    def remote(a, b, ss, rs, dev):
        return pltpu.make_async_remote_copy(
            src_ref=a, dst_ref=b, send_sem=ss, recv_sem=rs, device_id=dev, device_id_type=MESH)

    ez = select_matrix((lanes, nz), 0)
    ey = select_matrix((ny, cy), 1)
    rz = select_matrix((nz, lanes), 1)
    ry = select_matrix((cy, ny), 0)

    def expand(block):
        return dot(ey, dot(block, ez))

    def restrict_plane(total):
        return dot(dot(ry, total), rz) * F32(1.0 / 64.0)

    def lookup(lab, row):
        total = jnp.zeros(lab.shape, F32)
        for r in range(regions):
            total = total + jnp.where(lab == F32(r), row(r), F32(0.0))
        return total

    crow = lax.broadcasted_iota(jnp.int32, (cx, cy, lanes), 1)
    c_first, c_last = crow == 0, crow == cy - 1
    czero = jnp.zeros((1, cy, lanes), F32)

    def c_neighbours(w):
        total = jnp.concatenate([czero, w[:-1]], 0) + jnp.concatenate([w[1:], czero], 0)
        total = total + jnp.where(c_first, F32(0.0), pltpu.roll(w, 1, 1))
        total = total + jnp.where(c_last, F32(0.0), pltpu.roll(w, cy - 1, 1))
        return total + (pltpu.roll(w, 1, 2) + pltpu.roll(w, lanes - 1, 2))

    def c_jacobi(scaled, w, c_weight):
        for _ in range(C_SWEEPS):
            w = scaled + c_weight * c_neighbours(w)
        return w

    frow = lax.broadcasted_iota(jnp.int32, (ny, nz), 0)
    fcol = lax.broadcasted_iota(jnp.int32, (ny, nz), 1)
    y_first, y_last = frow == 0, frow == ny - 1
    z_first, z_last = fcol == 0, fcol == nz - 1

    def in_plane(w):
        a = jnp.where(y_first, F32(0.0), pltpu.roll(w, 1, 0))
        b = jnp.where(y_last, F32(0.0), pltpu.roll(w, ny - 1, 0))
        c = jnp.where(z_first, F32(0.0), pltpu.roll(w, 1, 1))
        d = jnp.where(z_last, F32(0.0), pltpu.roll(w, nz - 1, 1))
        return (a + b) + (c + d)

    def fine_step(first, length, shrink):
        def scale(q, _):
            p = first + q
            sc[p] = (u[p + 1] + src[p]) * inv[p]
            return 0
        lax.fori_loop(0, length, scale, 0)

        def sweep(i, _):
            cut = 2 * (i // 2)
            lo = first + cut

            def quad(q, carry):
                before, cur = carry
                for r in range(4):
                    p = lo + 4 * q + r
                    after = u[p + 2]
                    u[p + 1] = sc[p] + wt[p] * ((before + after) + in_plane(cur))
                    before, cur = cur, after
                return before, cur

            lax.fori_loop(0, (length - 2 * cut) // 4, quad, (u[lo], u[lo + 1]))
            return 0
        lax.fori_loop(0, shrink, sweep, 0)

    def gather_start(stage, ref, mine):
        copies = []
        for j in range(1, s_count):
            copy = remote(mine(ref), mine(ref), ag_ss.at[stage, j], ag_rs.at[stage, j],
                          (n, lax.rem(s + j, s_count)))
            copy.start()
            copies.append(copy)
        return copies

    own = pl.ds(pad + bx * s, bx)

    ext = W1 * 2 + planes
    zero_block = jnp.zeros((pad, cy, lanes), F32)
    for k in (0, pad + cx):
        ag[0, k:k + pad] = zero_block
        ag[1, k:k + pad] = zero_block - 1.0
        kp[k:k + pad] = zero_block
    zero_fine = jnp.zeros((ny, nz), F32)
    u[0] = zero_fine
    u[ext + 1] = zero_fine

    def restricted(plane_of, ref, lead):
        for k in range(bx):
            total = (plane_of(4 * k) + plane_of(4 * k + 1)) + (plane_of(4 * k + 2) + plane_of(4 * k + 3))
            value = restrict_plane(total)
            if lead:
                ref[0, pad + bx * s + k] = value
            else:
                ref[bx * s + k] = value

    restricted(lambda p: init[p], ag, True)
    lane_pad = jnp.full((bx, cy, lanes - cz), -1.0, F32)
    ag[1, own] = jnp.concatenate([labels[...].astype(F32), lane_pad], axis=2)
    g0 = gather_start(0, ag, lambda r: r.at[:, own])

    first_slice = n == 0
    ih_lo = remote(init, t0.at[pl.ds(W1 + planes, W1)], ih_ss.at[0], ih_rs.at[0], (n, s - 1))
    ih_hi = remote(init, t0.at[pl.ds(0, W1)], ih_ss.at[1], ih_rs.at[1], (n, s + 1))

    @pl.when(first_slice & has_lo)
    def _():
        ih_lo.start()

    @pl.when(first_slice & has_hi)
    def _():
        ih_hi.start()

    @pl.when(jnp.logical_not(has_lo))
    def _():
        t0[0:W1] = jnp.zeros((W1, ny, nz), F32)
        fr[0:W2] = jnp.zeros((W2, ny, nz), F32)
        mid[0] = jnp.zeros((W2, ny, nz), F32)

    @pl.when(jnp.logical_not(has_hi))
    def _():
        t0[W1 + planes:] = jnp.zeros((W1, ny, nz), F32)
        fr[W2 + planes:] = jnp.zeros((W2, ny, nz), F32)
        mid[1] = jnp.zeros((W2, ny, nz), F32)

    for copy in g0:
        copy.wait()

    def coeff(k, _):
        lab = ag[1, bx * s + k]
        rate = lookup(lab, lambda r: rates[0, r])
        iv = 1.0 / (1.0 + 6.0 * rate)
        we = rate * iv
        so = lookup(lab, lambda r: heat[n, r])
        fi, fw, fo = expand(iv), expand(we), expand(so)
        for r in range(4):
            inv[4 * k + r] = fi
            wt[4 * k + r] = fw
            src[4 * k + r] = fo
        return 0
    lax.fori_loop(0, ext // 4, coeff, 0)

    lab_all = ag[1, pad:pad + cx]
    c_rate = FINE_STEPS * lookup(lab_all, lambda r: rates[0, r]) / 16.0
    c_inv = 1.0 / (1.0 + 6.0 * c_rate)
    c_weight = c_rate * c_inv

    def advance(m, c):
        source = FINE_STEPS * lookup(lab_all, lambda r: heat[m, r])
        return c_jacobi((c + source) * c_inv, c, c_weight)

    own_c = lax.fori_loop(0, n, advance, ag[0, pad:pad + cx])
    dcur[...] = advance(n, own_c)
    kp[pad:pad + cx] = own_c

    @pl.when(first_slice)
    def _():
        @pl.when(has_hi)
        def _():
            ih_lo_wait = remote(init, t0.at[pl.ds(W1 + planes, W1)], ih_ss.at[0], ih_rs.at[0], (n, s + 1))
            ih_lo_wait.wait_recv()

        @pl.when(has_lo)
        def _():
            ih_hi_wait = remote(init, t0.at[pl.ds(0, W1)], ih_ss.at[1], ih_rs.at[1], (n, s - 1))
            ih_hi_wait.wait_recv()

        def lay(p, _):
            u[1 + p] = t0[p]
            u[1 + W1 + planes + p] = t0[W1 + planes + p]
            return 0
        lax.fori_loop(0, W1, lay, 0)

        def lay_own(p, _):
            u[1 + W1 + p] = init[p]
            return 0
        lax.fori_loop(0, planes, lay_own, 0)

    @pl.when(has_prev)
    def _():
        def lay(k, _):
            f = expand(kp[bx * s + k])
            for r in range(4):
                u[1 + 4 * k + r] = f
            return 0
        lax.fori_loop(0, ext // 4, lay, 0)

    fine_step(0, ext, SWEEPS)
    fine_step(SWEEPS, ext - 2 * SWEEPS, SWEEPS)

    own_g = pl.ds(bx * s, bx)

    def coarse_part(stage, plane_of):
        restricted(plane_of, gag.at[stage], False)
        copies = gather_start(stage + 1, gag.at[stage], lambda r: r.at[own_g])
        return copies

    def keep(p, _):
        fs[p] = u[1 + W1 + p]
        return 0
    lax.fori_loop(0, planes, keep, 0)
    g1 = coarse_part(0, lambda p: fs[p])

    f_own = remote(fs, fr.at[pl.ds(W2, planes)], f_ss.at[0], f_rs.at[0], (n + 1, s))
    f_lo = remote(fs.at[pl.ds(0, W2)], fr.at[pl.ds(W2 + planes, W2)], f_ss.at[1], f_rs.at[1], (n + 1, s - 1))
    f_hi = remote(fs.at[pl.ds(planes - W2, W2)], fr.at[pl.ds(0, W2)], f_ss.at[2], f_rs.at[2], (n + 1, s + 1))

    @pl.when(has_next)
    def _():
        f_own.start()

    @pl.when(has_next & has_lo)
    def _():
        f_lo.start()

    @pl.when(has_next & has_hi)
    def _():
        f_hi.start()

    for copy in g1:
        copy.wait()

    def chain(stage):
        e_copy = remote(es.at[stage], er.at[stage], e_ss.at[stage], e_rs.at[stage], (n + 1, s))

        @pl.when(first_slice)
        def _():
            er[stage] = jnp.zeros((cx, cy, lanes), F32)

        @pl.when(has_prev)
        def _():
            e_copy.wait_recv()
        e = er[stage]
        corr = c_jacobi(e * c_inv, e, c_weight)
        rf = gag[stage]
        es[stage] = corr + (rf - dcur[...])

        @pl.when(has_next)
        def _():
            e_copy.start()
        dcur[...] = rf + corr
        return corr

    cs[...] = chain(0)
    c_copy = remote(cs, cr, c_ss, c_rs, (n + 1, s))

    @pl.when(has_next)
    def _():
        c_copy.start()

    off = W1 - W2
    span = planes + 2 * W2

    @pl.when(first_slice)
    def _():
        def lay(p, _):
            u[1 + off + p] = t0[off + p]
            u[1 + W1 + planes + p] = t0[W1 + planes + p]
            return 0
        lax.fori_loop(0, W2, lay, 0)

        def lay_own(p, _):
            u[1 + W1 + p] = init[p]
            return 0
        lax.fori_loop(0, planes, lay_own, 0)

    @pl.when(has_prev)
    def _():
        c_copy.wait_recv()
        f_own.wait_recv()

        @pl.when(has_hi)
        def _():
            f_lo.wait_recv()

        @pl.when(has_lo)
        def _():
            f_hi.wait_recv()
        kp[pad:pad + cx] = cr[...]

        def lay(k, _):
            f = expand(kp[bx * s + off // 4 + k])
            for r in range(4):
                u[1 + off + 4 * k + r] = fr[4 * k + r] + f
            return 0
        lax.fori_loop(0, span // 4, lay, 0)

    fine_step(off, span, SWEEPS)

    m_lo = remote(u.at[pl.ds(1 + W1, W2)], mid.at[1], m_ss.at[0], m_rs.at[0], (n, s - 1))
    m_hi = remote(u.at[pl.ds(1 + W1 + planes - W2, W2)], mid.at[0], m_ss.at[1], m_rs.at[1], (n, s + 1))

    @pl.when(has_lo)
    def _():
        m_lo.start()

    @pl.when(has_hi)
    def _():
        m_hi.start()

    @pl.when(has_lo)
    def _():
        m_hi.wait_recv()
        m_lo.wait_send()

    @pl.when(has_hi)
    def _():
        m_lo.wait_recv()
        m_hi.wait_send()

    def lay_mid(p, _):
        u[1 + off + p] = mid[0, p]
        u[1 + W1 + planes + p] = mid[1, p]
        return 0
    lax.fori_loop(0, W2, lay_mid, 0)
    fine_step(off, span, SWEEPS)

    g2 = coarse_part(1, lambda p: u[1 + W1 + p])
    for copy in g2:
        copy.wait()
    kp[pad:pad + cx] = chain(1)

    def finish(k, _):
        f = expand(kp[pad + bx * s + k])
        for r in range(4):
            out[0, 4 * k + r] = u[1 + W1 + 4 * k + r] + f
        return 0
    lax.fori_loop(0, bx, finish, 0)

    @pl.when(first_slice & has_lo)
    def _():
        ih_lo.wait_send()

    @pl.when(first_slice & has_hi)
    def _():
        ih_hi.wait_send()

    @pl.when(has_next)
    def _():
        f_own.wait_send()
        c_copy.wait_send()
        for stage in range(2):
            remote(es.at[stage], er.at[stage], e_ss.at[stage], e_rs.at[stage], (n + 1, s)).wait_send()

    @pl.when(has_next & has_lo)
    def _():
        f_lo.wait_send()

    @pl.when(has_next & has_hi)
    def _():
        f_hi.wait_send()


def solution(mesh):
    n_count, s_count = mesh.shape["tm"], mesh.shape["space"]

    def on_device(init, labels, rates, heat):
        planes, ny, nz = init.shape
        bx, cy, cz = labels.shape
        cx = bx * s_count
        lanes = 128 * (cz // 128 + 1)
        pad = W1 // 4
        ext = planes + 2 * W1
        dma = pltpu.SemaphoreType.DMA

        def vm(*shape):
            return pltpu.VMEM(shape, F32)

        vmem = pl.BlockSpec(memory_space=pltpu.VMEM)
        smem = pl.BlockSpec(memory_space=pltpu.SMEM)
        return pl.pallas_call(
            functools.partial(kernel, n_count, s_count),
            out_shape=jax.ShapeDtypeStruct((1, planes, ny, nz), F32),
            in_specs=[vmem, vmem, smem, smem],
            out_specs=vmem,
            scratch_shapes=[
                vm(2, cx + 2 * pad, cy, lanes),
                vm(2, cx, cy, lanes),
                vm(ext, ny, nz),
                vm(ext + 2, ny, nz),
                vm(ext, ny, nz), vm(ext, ny, nz), vm(ext, ny, nz), vm(ext, ny, nz),
                vm(planes, ny, nz),
                vm(planes + 2 * W2, ny, nz),
                vm(2, W2, ny, nz),
                vm(cx + 2 * pad, cy, lanes),
                vm(2, cx, cy, lanes), vm(2, cx, cy, lanes),
                vm(cx, cy, lanes), vm(cx, cy, lanes), vm(cx, cy, lanes),
                dma((3, s_count)), dma((3, s_count)),
                dma((2,)), dma((2,)),
                dma((3,)), dma((3,)),
                dma((2,)), dma((2,)),
                dma((2,)), dma((2,)),
                dma(()), dma(()),
            ],
            compiler_params=pltpu.CompilerParams(
                collective_id=0, has_side_effects=True, vmem_limit_bytes=48 * 1024 * 1024),
            name="parareal",
        )(init, labels, rates.reshape(1, -1), heat)

    return jax.shard_map(
        on_device,
        mesh=mesh,
        in_specs=(P("space", None, None), P("space", None, None), P(), P()),
        out_specs=P("tm", "space", None, None),
        check_vma=False,
    )
```

time: 666 us -> 110 us (0.17); the launches traced: 652 us -> 110 us
  starting transfers between devices: 210 us -> 0 us
  waiting for transfers between devices: 195 us -> 0 us
  local copies, waits for them, and re-layouts: 177 us -> 3.89 us
  Pallas kernels: 0 us -> 106 us
  other arithmetic: 66.8 us -> 0 us
    ppermute x90 -> x0, starting transfers between devices: 210 us -> none  [the longest x34 112 us: with_halo(): after = lax.ppermute(initial, axis, down)]
    ppermute x90 -> x0, waiting for transfers between devices: 195 us -> none  [the longest x22 120 us: shifted(): return lax.ppermute(array, axis, pairs)]
    reshape x7 -> x0, local copies, waits for them, and re-layouts: 117 us -> none  [the longest x4 60.7 us: expand(): return wide.reshape((4 * sx, 4 * sy, 4 * sz))]
    pallas_call x0 -> x1, Pallas kernels: none -> 106 us  [on_device(): pl.pallas_call(functools.partial(kernel, n_count, s_count), out_shape=jax...]
    broadcast_in_dim x5 -> x0, local copies, waits for them, and re-layouts: 40 us -> none  [expand(): jnp.broadcast_to(block[:, None, :, None, :, None], (sx, 4, sy, 4, sz, 4))]
    add x152 -> x0, other arithmetic: 31.7 us -> none  [the longest x32 19.7 us: on_device(): fine_field_ext = fine_scaled + fine_coeffs[1] * neighbours(fine_field_ext)]
    reduce_sum x3 -> x0, other arithmetic: 21.1 us -> none  [restrict(): return jnp.mean(split, axis=(1, 3, 5))]
    another operation x1 -> x0, local copies, waits for them, and re-layouts: 15 us -> none  [on_device(): jnp.stack([inv_fine, weight_fine, source_fine])]
  transfers between devices with their start and end apart: 90 -> 0, of which waited for: 61 -> 0; matrix products, arithmetic and copies ran while one was open for 15% -> 0% of each run, Pallas kernels for 0% -> 0%
where the time goes in v1:
time: 110 us
  Pallas kernels  106 us (96%)
  local copies, waits for them, and re-layouts  3.89 us (4%)
    pallas_call x1, Pallas kernels, on_device(): pl.pallas_call(functools.partial(kernel, n_count, s_count), out_shape=jax...  106 us
    unnamed x9, local copies, waits for them, and re-layouts  3.89 us

profile of v1, /device:TPU:27, one launch (start us, length us, event | category | flops | bytes accessed | tf_op | source)
XLA Modules:
  0.0 109.6 jit_solution(13124872866778144735)
XLA Ops:
  0.0 0.0 copy-start.3
  0.0 0.7 copy-done.3
  0.7 0.0 copy-start
  0.7 1.0 copy-done
  1.7 0.0 copy-start.1
  1.7 0.7 copy-done.1
  2.4 0.0 copy-start.2
  2.4 0.7 copy-done.2
  3.1 105.7 %parareal.1 = f32[1,16,32,256]{3,2,1,0:T(8,128)S(1)} custom-call(f32[16,32,256]{2,1,0:T(8,128)S(1)} %copy-done, s32[4,8,64]{2,1,0:T(8,128)S(1)} %copy-done.1, f32[1,6]{1,0:T(1,128)S(1)} %bitcast.1, f32[8,6]{1,0:T(8,128)S(1)} %copy-done.2), custom_call_target="tpu_custom_call" | custom-call | tf_op jit(solution)/shard_map/parareal/pallas_call | solution.py:443
  108.8 0.8 copy.6
Async XLA Ops:
  0.0 0.7 copy-start.3
  0.7 1.0 copy-start
  1.7 0.7 copy-start.1
  2.4 0.7 copy-start.2

commit v2 on v1

--- a/solution.py
+++ b/solution.py
@@ -21,30 +21,30 @@
     return jnp.dot(a, b, precision=HI, preferred_element_type=F32)
 
 
-def select_matrix(shape, small_axis):
-    small = lax.broadcasted_iota(jnp.int32, shape, small_axis)
-    large = lax.broadcasted_iota(jnp.int32, shape, 1 - small_axis)
-    hit = (large >= 4 * small) & (large < 4 * small + 4)
-    return jnp.where(hit, F32(1.0), F32(0.0))
-
-
 def kernel(
     n_count, s_count,
-    init, labels, rates, heat,
+    init_hbm, labels_hbm, rates_hbm, heat_hbm,
     out,
+    raw, labels, rates, heat, in_sem, init,
     ag, gag, t0, u, sc, wt, inv, src, fs, fr, mid, kp, es, er, cs, cr, dcur,
     ag_ss, ag_rs, ih_ss, ih_rs, f_ss, f_rs, m_ss, m_rs, e_ss, e_rs, c_ss, c_rs,
 ):
     n = lax.axis_index("tm")
     s = lax.axis_index("space")
-    planes, ny, nz = init.shape
-    bx, cy, cz = labels.shape
+    planes, ny, nz = init_hbm.shape
+    bx, cy, cz = labels_hbm.shape
     cx = bx * s_count
     lanes = ag.shape[-1]
-    regions = rates.shape[1]
+    ts, zs = ny // cy, nz // lanes
+    regions = rates_hbm.shape[1]
     pad = W1 // 4
     has_prev, has_next = n > 0, n < n_count - 1
     has_lo, has_hi = s > 0, s < s_count - 1
+
+    fetches = [pltpu.make_async_copy(a, b, in_sem.at[i]) for i, (a, b) in enumerate(
+        ((init_hbm, raw), (labels_hbm, labels), (rates_hbm, rates), (heat_hbm, heat)))]
+    for fetch in fetches:
+        fetch.start()
 
     barrier = pltpu.get_barrier_semaphore()
     def greet(cond, dev):
@@ -68,16 +68,23 @@
         return pltpu.make_async_remote_copy(
             src_ref=a, dst_ref=b, send_sem=ss, recv_sem=rs, device_id=dev, device_id_type=MESH)
 
-    ez = select_matrix((lanes, nz), 0)
-    ey = select_matrix((ny, cy), 1)
-    rz = select_matrix((nz, lanes), 1)
-    ry = select_matrix((cy, ny), 0)
-
-    def expand(block):
-        return dot(ey, dot(block, ez))
-
-    def restrict_plane(total):
-        return dot(dot(ry, total), rz) * F32(1.0 / 64.0)
+    half = 4 // zs
+
+    def restrict(planes4):
+        total = planes4[0]
+        for extra in planes4[1:]:
+            total = total + extra
+        part = total[0]
+        for k in range(1, ts * zs):
+            part = part + total[k]
+        lane = lax.broadcasted_iota(jnp.int32, part.shape, 1)
+        step = 1
+        while step < half:
+            swap = jnp.where(lane % (2 * step) < step,
+                             pltpu.roll(part, lanes - step, 1), pltpu.roll(part, step, 1))
+            part = part + swap
+            step *= 2
+        return part * F32(1.0 / 64.0)
 
     def lookup(lab, row):
         total = jnp.zeros(lab.shape, F32)
@@ -86,53 +93,78 @@
         return total
 
     crow = lax.broadcasted_iota(jnp.int32, (cx, cy, lanes), 1)
+    ccol = lax.broadcasted_iota(jnp.int32, (cx, cy, lanes), 2)
     c_first, c_last = crow == 0, crow == cy - 1
+    cz_first, cz_last = ccol < half, ccol >= lanes - half
     czero = jnp.zeros((1, cy, lanes), F32)
 
     def c_neighbours(w):
         total = jnp.concatenate([czero, w[:-1]], 0) + jnp.concatenate([w[1:], czero], 0)
-        total = total + jnp.where(c_first, F32(0.0), pltpu.roll(w, 1, 1))
-        total = total + jnp.where(c_last, F32(0.0), pltpu.roll(w, cy - 1, 1))
-        return total + (pltpu.roll(w, 1, 2) + pltpu.roll(w, lanes - 1, 2))
+        total = total + (jnp.where(c_first, F32(0.0), pltpu.roll(w, 1, 1))
+                         + jnp.where(c_last, F32(0.0), pltpu.roll(w, cy - 1, 1)))
+        return total + (jnp.where(cz_first, F32(0.0), pltpu.roll(w, half, 2))
+                        + jnp.where(cz_last, F32(0.0), pltpu.roll(w, lanes - half, 2)))
 
     def c_jacobi(scaled, w, c_weight):
         for _ in range(C_SWEEPS):
             w = scaled + c_weight * c_neighbours(w)
         return w
 
-    frow = lax.broadcasted_iota(jnp.int32, (ny, nz), 0)
-    fcol = lax.broadcasted_iota(jnp.int32, (ny, nz), 1)
-    y_first, y_last = frow == 0, frow == ny - 1
-    z_first, z_last = fcol == 0, fcol == nz - 1
-
-    def in_plane(w):
-        a = jnp.where(y_first, F32(0.0), pltpu.roll(w, 1, 0))
-        b = jnp.where(y_last, F32(0.0), pltpu.roll(w, ny - 1, 0))
-        c = jnp.where(z_first, F32(0.0), pltpu.roll(w, 1, 1))
-        d = jnp.where(z_last, F32(0.0), pltpu.roll(w, nz - 1, 1))
-        return (a + b) + (c + d)
+    row = lax.broadcasted_iota(jnp.int32, (cy, lanes), 0)
+    col = lax.broadcasted_iota(jnp.int32, (cy, lanes), 1)
+    y_first, y_last = row == 0, row == cy - 1
+    z_first, z_last = col == 0, col == lanes - 1
+
+    def in_plane(w, k):
+        t, c = k // zs, k % zs
+        if t > 0:
+            a = w[k - zs]
+        else:
+            a = jnp.where(y_first, F32(0.0), pltpu.roll(w[(ts - 1) * zs + c], 1, 0))
+        if t < ts - 1:
+            b = w[k + zs]
+        else:
+            b = jnp.where(y_last, F32(0.0), pltpu.roll(w[c], cy - 1, 0))
+        if c > 0:
+            d = w[k - 1]
+        else:
+            d = jnp.where(z_first, F32(0.0), pltpu.roll(w[k + zs - 1], 1, 1))
+        if c < zs - 1:
+            e = w[k + 1]
+        else:
+            e = jnp.where(z_last, F32(0.0), pltpu.roll(w[k - zs + 1], lanes - 1, 1))
+        return (a + b) + (d + e)
+
+    tiles = ts * zs
 
     def fine_step(first, length, shrink):
         def scale(q, _):
-            p = first + q
-            sc[p] = (u[p + 1] + src[p]) * inv[p]
-            return 0
-        lax.fori_loop(0, length, scale, 0)
+            g = first // 4 + q
+            iv, so = inv[g], src[g]
+            for r in range(4):
+                p = first + 4 * q + r
+                for k in range(tiles):
+                    sc[p, k] = (u[p + 1, k] + so) * iv
+            return 0
+        lax.fori_loop(0, length // 4, scale, 0)
 
         def sweep(i, _):
-            cut = 2 * (i // 2)
+            cut = 4 * (i // 4)
             lo = first + cut
 
             def quad(q, carry):
                 before, cur = carry
+                we = wt[lo // 4 + q]
                 for r in range(4):
                     p = lo + 4 * q + r
-                    after = u[p + 2]
-                    u[p + 1] = sc[p] + wt[p] * ((before + after) + in_plane(cur))
+                    after = [u[p + 2, k] for k in range(tiles)]
+                    for k in range(tiles):
+                        u[p + 1, k] = sc[p, k] + we * ((before[k] + after[k]) + in_plane(cur, k))
                     before, cur = cur, after
                 return before, cur
 
-            lax.fori_loop(0, (length - 2 * cut) // 4, quad, (u[lo], u[lo + 1]))
+            lax.fori_loop(0, (length - 2 * cut) // 4, quad,
+                          ([u[lo, k] for k in range(tiles)], [u[lo + 1, k] for k in range(tiles)]))
             return 0
         lax.fori_loop(0, shrink, sweep, 0)
 
@@ -153,22 +185,38 @@
         ag[0, k:k + pad] = zero_block
         ag[1, k:k + pad] = zero_block - 1.0
         kp[k:k + pad] = zero_block
-    zero_fine = jnp.zeros((ny, nz), F32)
+    def zeros(*lead):
+        return jnp.zeros(lead + (tiles, cy, lanes), F32)
+
+    zero_fine = zeros()
     u[0] = zero_fine
     u[ext + 1] = zero_fine
 
-    def restricted(plane_of, ref, lead):
-        for k in range(bx):
-            total = (plane_of(4 * k) + plane_of(4 * k + 1)) + (plane_of(4 * k + 2) + plane_of(4 * k + 3))
-            value = restrict_plane(total)
-            if lead:
-                ref[0, pad + bx * s + k] = value
-            else:
-                ref[bx * s + k] = value
-
-    restricted(lambda p: init[p], ag, True)
-    lane_pad = jnp.full((bx, cy, lanes - cz), -1.0, F32)
-    ag[1, own] = jnp.concatenate([labels[...].astype(F32), lane_pad], axis=2)
+    for fetch in fetches:
+        fetch.wait()
+
+    zi = lax.broadcasted_iota(jnp.int32, (nz, nz), 0)
+    zj = lax.broadcasted_iota(jnp.int32, (nz, nz), 1)
+    to_tiles = jnp.where(zi == zs * (zj % lanes) + zj // lanes, F32(1.0), F32(0.0))
+
+    yi = lax.broadcasted_iota(jnp.int32, (ny, ny), 0)
+    yj = lax.broadcasted_iota(jnp.int32, (ny, ny), 1)
+    rows_to_tiles = jnp.where(yj == ts * (yi % cy) + yi // cy, F32(1.0), F32(0.0))
+
+    def load(p, _):
+        moved = dot(rows_to_tiles, dot(raw[p], to_tiles))
+        for t in range(ts):
+            for c in range(zs):
+                init[p, t * zs + c] = moved[t * cy:(t + 1) * cy, c * lanes:(c + 1) * lanes]
+        return 0
+    lax.fori_loop(0, planes, load, 0, unroll=2)
+
+    li = lax.broadcasted_iota(jnp.int32, (cz, lanes), 0)
+    lj = lax.broadcasted_iota(jnp.int32, (cz, lanes), 1)
+    spread = jnp.where(li == lj // half, F32(1.0), F32(0.0))
+    for k in range(bx):
+        ag[0, pad + bx * s + k] = restrict([init[4 * k + r] for r in range(4)])
+        ag[1, pad + bx * s + k] = dot(labels[k].astype(F32), spread)
     g0 = gather_start(0, ag, lambda r: r.at[:, own])
 
     first_slice = n == 0
@@ -185,32 +233,25 @@
 
     @pl.when(jnp.logical_not(has_lo))
     def _():
-        t0[0:W1] = jnp.zeros((W1, ny, nz), F32)
-        fr[0:W2] = jnp.zeros((W2, ny, nz), F32)
-        mid[0] = jnp.zeros((W2, ny, nz), F32)
+        t0[0:W1] = zeros(W1)
+        fr[0:W2] = zeros(W2)
+        mid[0] = zeros(W2)
 
     @pl.when(jnp.logical_not(has_hi))
     def _():
-        t0[W1 + planes:] = jnp.zeros((W1, ny, nz), F32)
-        fr[W2 + planes:] = jnp.zeros((W2, ny, nz), F32)
-        mid[1] = jnp.zeros((W2, ny, nz), F32)
+        t0[W1 + planes:] = zeros(W1)
+        fr[W2 + planes:] = zeros(W2)
+        mid[1] = zeros(W2)
 
     for copy in g0:
         copy.wait()
 
-    def coeff(k, _):
-        lab = ag[1, bx * s + k]
-        rate = lookup(lab, lambda r: rates[0, r])
-        iv = 1.0 / (1.0 + 6.0 * rate)
-        we = rate * iv
-        so = lookup(lab, lambda r: heat[n, r])
-        fi, fw, fo = expand(iv), expand(we), expand(so)
-        for r in range(4):
-            inv[4 * k + r] = fi
-            wt[4 * k + r] = fw
-            src[4 * k + r] = fo
-        return 0
-    lax.fori_loop(0, ext // 4, coeff, 0)
+    lab = ag[1, pl.ds(bx * s, ext // 4)]
+    rate = lookup(lab, lambda r: rates[0, r])
+    iv = 1.0 / (1.0 + 6.0 * rate)
+    inv[...] = iv
+    wt[...] = rate * iv
+    src[...] = lookup(lab, lambda r: heat[n, r])
 
     lab_all = ag[1, pad:pad + cx]
     c_rate = FINE_STEPS * lookup(lab_all, lambda r: rates[0, r]) / 16.0
@@ -251,9 +292,10 @@
     @pl.when(has_prev)
     def _():
         def lay(k, _):
-            f = expand(kp[bx * s + k])
+            f = kp[bx * s + k]
             for r in range(4):
-                u[1 + 4 * k + r] = f
+                for q in range(tiles):
+                    u[1 + 4 * k + r, q] = f
             return 0
         lax.fori_loop(0, ext // 4, lay, 0)
 
@@ -263,7 +305,8 @@
     own_g = pl.ds(bx * s, bx)
 
     def coarse_part(stage, plane_of):
-        restricted(plane_of, gag.at[stage], False)
+        for k in range(bx):
+            gag[stage, bx * s + k] = restrict([plane_of(4 * k + r) for r in range(4)])
         copies = gather_start(stage + 1, gag.at[stage], lambda r: r.at[own_g])
         return copies
 
@@ -351,9 +394,10 @@
         kp[pad:pad + cx] = cr[...]
 
         def lay(k, _):
-            f = expand(kp[bx * s + off // 4 + k])
+            f = kp[bx * s + off // 4 + k]
             for r in range(4):
-                u[1 + off + 4 * k + r] = fr[4 * k + r] + f
+                for q in range(tiles):
+                    u[1 + off + 4 * k + r, q] = fr[4 * k + r, q] + f
             return 0
         lax.fori_loop(0, span // 4, lay, 0)
 
@@ -392,12 +436,18 @@
         copy.wait()
     kp[pad:pad + cx] = chain(1)
 
-    def finish(k, _):
-        f = expand(kp[pad + bx * s + k])
-        for r in range(4):
-            out[0, 4 * k + r] = u[1 + W1 + 4 * k + r] + f
+    from_tiles = jnp.where(zj == zs * (zi % lanes) + zi // lanes, F32(1.0), F32(0.0))
+
+    rows_from_tiles = jnp.where(yi == ts * (yj % cy) + yj // cy, F32(1.0), F32(0.0))
+
+    def finish(p, _):
+        f = kp[pad + bx * s + p // 4]
+        w = u[1 + W1 + p]
+        rows = jnp.concatenate(
+            [jnp.concatenate([w[t * zs + c] + f for c in range(zs)], 1) for t in range(ts)], 0)
+        out[0, p] = dot(rows_from_tiles, dot(rows, from_tiles))
         return 0
-    lax.fori_loop(0, bx, finish, 0)
+    lax.fori_loop(0, planes, finish, 0, unroll=2)
 
     @pl.when(first_slice & has_lo)
     def _():
@@ -430,7 +480,8 @@
         planes, ny, nz = init.shape
         bx, cy, cz = labels.shape
         cx = bx * s_count
-        lanes = 128 * (cz // 128 + 1)
+        lanes = 128
+        tile = (ny * nz // (cy * lanes), cy, lanes)
         pad = W1 // 4
         ext = planes + 2 * W1
         dma = pltpu.SemaphoreType.DMA
@@ -439,21 +490,23 @@
             return pltpu.VMEM(shape, F32)
 
         vmem = pl.BlockSpec(memory_space=pltpu.VMEM)
-        smem = pl.BlockSpec(memory_space=pltpu.SMEM)
         return pl.pallas_call(
             functools.partial(kernel, n_count, s_count),
             out_shape=jax.ShapeDtypeStruct((1, planes, ny, nz), F32),
-            in_specs=[vmem, vmem, smem, smem],
+            in_specs=[pl.BlockSpec(memory_space=pl.ANY)] * 4,
             out_specs=vmem,
             scratch_shapes=[
+                vm(*init.shape), pltpu.VMEM(labels.shape, labels.dtype),
+                pltpu.SMEM((1, rates.shape[0]), F32), pltpu.SMEM(heat.shape, F32),
+                dma((4,)), vm(planes, *tile),
                 vm(2, cx + 2 * pad, cy, lanes),
                 vm(2, cx, cy, lanes),
-                vm(ext, ny, nz),
-                vm(ext + 2, ny, nz),
-                vm(ext, ny, nz), vm(ext, ny, nz), vm(ext, ny, nz), vm(ext, ny, nz),
-                vm(planes, ny, nz),
-                vm(planes + 2 * W2, ny, nz),
-                vm(2, W2, ny, nz),
+                vm(ext, *tile),
+                vm(ext + 2, *tile),
+                vm(ext, *tile), vm(ext // 4, cy, lanes), vm(ext // 4, cy, lanes), vm(ext // 4, cy, lanes),
+                vm(planes, *tile),
+                vm(planes + 2 * W2, *tile),
+                vm(2, W2, *tile),
                 vm(cx + 2 * pad, cy, lanes),
                 vm(2, cx, cy, lanes), vm(2, cx, cy, lanes),
                 vm(cx, cy, lanes), vm(cx, cy, lanes), vm(cx, cy, lanes),

time: 110 us -> 100 us (0.909)
  Pallas kernels: 106 us -> 96.1 us
    pallas_call x1, Pallas kernels: 106 us -> 96.1 us  [on_device(): pl.pallas_call(functools.partial(kernel, n_count, s_count), out_shape=jax...]
where the time goes in v2:
time: 100 us
  Pallas kernels  96.1 us (96%)
  local copies, waits for them, and re-layouts  3.89 us (4%)
    pallas_call x1, Pallas kernels, on_device(): pl.pallas_call(functools.partial(kernel, n_count, s_count), out_shape=jax...  96.1 us
    unnamed x9, local copies, waits for them, and re-layouts  3.89 us

profile of v2, /device:TPU:27, one launch (start us, length us, event | category | flops | bytes accessed | tf_op | source)
XLA Modules:
  0.0 100.0 jit_solution(17298503133031295821)
XLA Ops:
  0.0 0.0 copy-start.3
  0.0 0.7 copy-done.3
  0.7 0.0 copy-start
  0.7 1.0 %copy-done = f32[16,32,256]{2,1,0:T(8,128)S(1)} copy-done((f32[16,32,256]{2,1,0:T(8,128)S(1)}, f32[16,32,256]{2,1,0:T(8,128)}, u32[]{:S(2)}) %copy-start) | copy-done | bytes 524312
  1.7 0.0 copy-start.1
  1.7 0.7 copy-done.1
  2.4 0.0 copy-start.2
  2.4 0.7 copy-done.2
  3.1 96.1 %parareal.1 = f32[1,16,32,256]{3,2,1,0:T(8,128)S(1)} custom-call(f32[16,32,256]{2,1,0:T(8,128)S(1)} %copy-done, s32[4,8,64]{2,1,0:T(8,128)S(1)} %copy-done.1, f32[1,6]{1,0:T(1,128)S(1)} %bitcast.1, f32[8,6]{1,0:T(8,128)S(1)} %copy-done.2), custom_call_target="tpu_custom_call" | custom-call | tf_op jit(solution)/shard_map/parareal/pallas_call | solution.py:493
  99.2 0.8 copy.6
Async XLA Ops:
  0.0 0.7 copy-start.3
  0.7 1.0 %copy-start = (f32[16,32,256]{2,1,0:T(8,128)S(1)}, f32[16,32,256]{2,1,0:T(8,128)}, u32[]{:S(2)}) copy-start(f32[16,32,256]{2,1,0:T(8,128)} %init_hbm.1) | copy-start | bytes 1572868
  1.7 0.7 copy-start.1
  2.4 0.7 copy-start.2

commit v3 on v2

--- a/solution.py
+++ b/solution.py
@@ -11,7 +11,7 @@
 SWEEPS = 8
 C_SWEEPS = 4
 W1 = FINE_STEPS * SWEEPS
-W2 = SWEEPS
+EW = 2 * W1
 F32 = jnp.float32
 MESH = pl.DeviceIdType.MESH
 HI = lax.Precision.HIGHEST
@@ -26,8 +26,8 @@
     init_hbm, labels_hbm, rates_hbm, heat_hbm,
     out,
     raw, labels, rates, heat, in_sem, init,
-    ag, gag, t0, u, sc, wt, inv, src, fs, fr, mid, kp, es, er, cs, cr, dcur,
-    ag_ss, ag_rs, ih_ss, ih_rs, f_ss, f_rs, m_ss, m_rs, e_ss, e_rs, c_ss, c_rs,
+    ag, gag, t0, u, sc, wt, inv, src, fs, fr, kp, es, er, cs, cr, dcur,
+    ag_ss, ag_rs, ih_ss, ih_rs, f_ss, f_rs, e_ss, e_rs, c_ss, c_rs,
 ):
     n = lax.axis_index("tm")
     s = lax.axis_index("space")
@@ -37,7 +37,7 @@
     lanes = ag.shape[-1]
     ts, zs = ny // cy, nz // lanes
     regions = rates_hbm.shape[1]
-    pad = W1 // 4
+    pad = EW // 4
     has_prev, has_next = n > 0, n < n_count - 1
     has_lo, has_hi = s > 0, s < s_count - 1
 
@@ -58,8 +58,9 @@
             barrier, inc=1, device_id=(n, lax.rem(s + j, s_count)), device_id_type=MESH)
     partners = s_count - 1
     for cond_n, dn in ((has_prev, -1), (has_next, 1)):
+        edge = n == (1 if dn < 0 else 0)
         for cond_s, ds in ((None, 0), (has_lo, -1), (has_hi, 1)):
-            cond = cond_n if cond_s is None else cond_n & cond_s
+            cond = cond_n if cond_s is None else cond_n & cond_s & edge
             greet(cond, (n + dn, s + ds))
             partners = partners + one(cond)
     pl.semaphore_wait(barrier, partners)
@@ -179,7 +180,9 @@
 
     own = pl.ds(pad + bx * s, bx)
 
-    ext = W1 * 2 + planes
+    ext = EW * 2 + planes
+    span = W1 * 2 + planes
+    off = EW - W1
     zero_block = jnp.zeros((pad, cy, lanes), F32)
     for k in (0, pad + cx):
         ag[0, k:k + pad] = zero_block
@@ -231,17 +234,23 @@
     def _():
         ih_hi.start()
 
-    @pl.when(jnp.logical_not(has_lo))
+    second_slice = n == 1
+
+    @pl.when(first_slice & jnp.logical_not(has_lo))
     def _():
         t0[0:W1] = zeros(W1)
-        fr[0:W2] = zeros(W2)
-        mid[0] = zeros(W2)
-
-    @pl.when(jnp.logical_not(has_hi))
+
+    @pl.when(first_slice & jnp.logical_not(has_hi))
     def _():
         t0[W1 + planes:] = zeros(W1)
-        fr[W2 + planes:] = zeros(W2)
-        mid[1] = zeros(W2)
+
+    @pl.when(second_slice & jnp.logical_not(has_lo))
+    def _():
+        fr[0:W1] = zeros(W1)
+
+    @pl.when(second_slice & jnp.logical_not(has_hi))
+    def _():
+        fr[W1 + planes:] = zeros(W1)
 
     for copy in g0:
         copy.wait()
@@ -279,13 +288,15 @@
             ih_hi_wait.wait_recv()
 
         def lay(p, _):
-            u[1 + p] = t0[p]
-            u[1 + W1 + planes + p] = t0[W1 + planes + p]
+            u[1 + off + p] = t0[p]
+            u[1 + EW + planes + p] = t0[W1 + planes + p]
             return 0
         lax.fori_loop(0, W1, lay, 0)
+        u[off] = zero_fine
+        u[off + span + 1] = zero_fine
 
         def lay_own(p, _):
-            u[1 + W1 + p] = init[p]
+            u[1 + EW + p] = init[p]
             return 0
         lax.fori_loop(0, planes, lay_own, 0)
 
@@ -299,8 +310,10 @@
             return 0
         lax.fori_loop(0, ext // 4, lay, 0)
 
-    fine_step(0, ext, SWEEPS)
-    fine_step(SWEEPS, ext - 2 * SWEEPS, SWEEPS)
+    begin = jnp.where(first_slice, off, 0)
+    size = jnp.where(first_slice, span, ext)
+    fine_step(begin, size, SWEEPS)
+    fine_step(begin + SWEEPS, size - 2 * SWEEPS, SWEEPS)
 
     own_g = pl.ds(bx * s, bx)
 
@@ -310,27 +323,34 @@
         copies = gather_start(stage + 1, gag.at[stage], lambda r: r.at[own_g])
         return copies
 
+    g1 = coarse_part(0, lambda p: u[1 + EW + p])
+
     def keep(p, _):
-        fs[p] = u[1 + W1 + p]
+        fs[p] = u[1 + off + p]
         return 0
-    lax.fori_loop(0, planes, keep, 0)
-    g1 = coarse_part(0, lambda p: fs[p])
-
-    f_own = remote(fs, fr.at[pl.ds(W2, planes)], f_ss.at[0], f_rs.at[0], (n + 1, s))
-    f_lo = remote(fs.at[pl.ds(0, W2)], fr.at[pl.ds(W2 + planes, W2)], f_ss.at[1], f_rs.at[1], (n + 1, s - 1))
-    f_hi = remote(fs.at[pl.ds(planes - W2, W2)], fr.at[pl.ds(0, W2)], f_ss.at[2], f_rs.at[2], (n + 1, s + 1))
-
-    @pl.when(has_next)
+    lax.fori_loop(0, span, keep, 0)
+
+    own_part = pl.ds(W1, planes)
+    f_all = remote(fs, fr, f_ss.at[0], f_rs.at[0], (n + 1, s))
+    f_own = remote(fs.at[own_part], fr.at[own_part], f_ss.at[0], f_rs.at[0], (n + 1, s))
+    f_lo = remote(fs.at[own_part], fr.at[pl.ds(W1 + planes, W1)], f_ss.at[1], f_rs.at[1], (n + 1, s - 1))
+    f_hi = remote(fs.at[own_part], fr.at[pl.ds(0, W1)], f_ss.at[2], f_rs.at[2], (n + 1, s + 1))
+
+    @pl.when(first_slice & has_lo)
+    def _():
+        f_lo.start()
+
+    @pl.when(first_slice & has_hi)
+    def _():
+        f_hi.start()
+
+    @pl.when(first_slice & has_next)
     def _():
         f_own.start()
 
-    @pl.when(has_next & has_lo)
-    def _():
-        f_lo.start()
-
-    @pl.when(has_next & has_hi)
-    def _():
-        f_hi.start()
+    @pl.when(has_prev & has_next)
+    def _():
+        f_all.start()
 
     for copy in g1:
         copy.wait()
@@ -363,34 +383,25 @@
     def _():
         c_copy.start()
 
-    off = W1 - W2
-    span = planes + 2 * W2
-
-    @pl.when(first_slice)
-    def _():
-        def lay(p, _):
-            u[1 + off + p] = t0[off + p]
-            u[1 + W1 + planes + p] = t0[W1 + planes + p]
-            return 0
-        lax.fori_loop(0, W2, lay, 0)
-
-        def lay_own(p, _):
-            u[1 + W1 + p] = init[p]
-            return 0
-        lax.fori_loop(0, planes, lay_own, 0)
+    @pl.when(second_slice)
+    def _():
+        f_own.wait_recv()
+
+        @pl.when(has_hi)
+        def _():
+            f_lo.wait_recv()
+
+        @pl.when(has_lo)
+        def _():
+            f_hi.wait_recv()
+
+    @pl.when(n > 1)
+    def _():
+        f_all.wait_recv()
 
     @pl.when(has_prev)
     def _():
         c_copy.wait_recv()
-        f_own.wait_recv()
-
-        @pl.when(has_hi)
-        def _():
-            f_lo.wait_recv()
-
-        @pl.when(has_lo)
-        def _():
-            f_hi.wait_recv()
         kp[pad:pad + cx] = cr[...]
 
         def lay(k, _):
@@ -400,38 +411,10 @@
                     u[1 + off + 4 * k + r, q] = fr[4 * k + r, q] + f
             return 0
         lax.fori_loop(0, span // 4, lay, 0)
-
-    fine_step(off, span, SWEEPS)
-
-    m_lo = remote(u.at[pl.ds(1 + W1, W2)], mid.at[1], m_ss.at[0], m_rs.at[0], (n, s - 1))
-    m_hi = remote(u.at[pl.ds(1 + W1 + planes - W2, W2)], mid.at[0], m_ss.at[1], m_rs.at[1], (n, s + 1))
-
-    @pl.when(has_lo)
-    def _():
-        m_lo.start()
-
-    @pl.when(has_hi)
-    def _():
-        m_hi.start()
-
-    @pl.when(has_lo)
-    def _():
-        m_hi.wait_recv()
-        m_lo.wait_send()
-
-    @pl.when(has_hi)
-    def _():
-        m_lo.wait_recv()
-        m_hi.wait_send()
-
-    def lay_mid(p, _):
-        u[1 + off + p] = mid[0, p]
-        u[1 + W1 + planes + p] = mid[1, p]
-        return 0
-    lax.fori_loop(0, W2, lay_mid, 0)
-    fine_step(off, span, SWEEPS)
-
-    g2 = coarse_part(1, lambda p: u[1 + W1 + p])
+        fine_step(off, span, SWEEPS)
+        fine_step(off + SWEEPS, span - 2 * SWEEPS, SWEEPS)
+
+    g2 = coarse_part(1, lambda p: u[1 + EW + p])
     for copy in g2:
         copy.wait()
     kp[pad:pad + cx] = chain(1)
@@ -442,7 +425,7 @@
 
     def finish(p, _):
         f = kp[pad + bx * s + p // 4]
-        w = u[1 + W1 + p]
+        w = u[1 + EW + p]
         rows = jnp.concatenate(
             [jnp.concatenate([w[t * zs + c] + f for c in range(zs)], 1) for t in range(ts)], 0)
         out[0, p] = dot(rows_from_tiles, dot(rows, from_tiles))
@@ -459,16 +442,23 @@
 
     @pl.when(has_next)
     def _():
-        f_own.wait_send()
         c_copy.wait_send()
         for stage in range(2):
             remote(es.at[stage], er.at[stage], e_ss.at[stage], e_rs.at[stage], (n + 1, s)).wait_send()
 
-    @pl.when(has_next & has_lo)
+    @pl.when(has_prev & has_next)
+    def _():
+        f_all.wait_send()
+
+    @pl.when(first_slice & has_next)
+    def _():
+        f_own.wait_send()
+
+    @pl.when(first_slice & has_lo)
     def _():
         f_lo.wait_send()
 
-    @pl.when(has_next & has_hi)
+    @pl.when(first_slice & has_hi)
     def _():
         f_hi.wait_send()
 
@@ -482,8 +472,9 @@
         cx = bx * s_count
         lanes = 128
         tile = (ny * nz // (cy * lanes), cy, lanes)
-        pad = W1 // 4
-        ext = planes + 2 * W1
+        pad = EW // 4
+        ext = planes + 2 * EW
+        span = planes + 2 * W1
         dma = pltpu.SemaphoreType.DMA
 
         def vm(*shape):
@@ -501,12 +492,11 @@
                 dma((4,)), vm(planes, *tile),
                 vm(2, cx + 2 * pad, cy, lanes),
                 vm(2, cx, cy, lanes),
-                vm(ext, *tile),
+                vm(span, *tile),
                 vm(ext + 2, *tile),
                 vm(ext, *tile), vm(ext // 4, cy, lanes), vm(ext // 4, cy, lanes), vm(ext // 4, cy, lanes),
-                vm(planes, *tile),
-                vm(planes + 2 * W2, *tile),
-                vm(2, W2, *tile),
+                vm(span, *tile),
+                vm(span, *tile),
                 vm(cx + 2 * pad, cy, lanes),
                 vm(2, cx, cy, lanes), vm(2, cx, cy, lanes),
                 vm(cx, cy, lanes), vm(cx, cy, lanes), vm(cx, cy, lanes),
@@ -514,7 +504,6 @@
                 dma((2,)), dma((2,)),
                 dma((3,)), dma((3,)),
                 dma((2,)), dma((2,)),
-                dma((2,)), dma((2,)),
                 dma(()), dma(()),
             ],
             compiler_params=pltpu.CompilerParams(

time: 100 us -> 105 us (1.050)
  Pallas kernels: 96.1 us -> 101 us
    pallas_call x1, Pallas kernels: 96.1 us -> 101 us  [on_device(): pl.pallas_call(functools.partial(kernel, n_count, s_count), out_shape=jax...]
where the time goes in v3:
time: 105 us
  Pallas kernels  101 us (96%)
  local copies, waits for them, and re-layouts  3.89 us (4%)
    pallas_call x1, Pallas kernels, on_device(): pl.pallas_call(functools.partial(kernel, n_count, s_count), out_shape=jax...  101 us
    unnamed x9, local copies, waits for them, and re-layouts  3.89 us

profile of v3, /device:TPU:27, one launch (start us, length us, event | category | flops | bytes accessed | tf_op | source)
XLA Modules:
  0.0 104.8 jit_solution(7022573782279974224)
XLA Ops:
  0.0 0.0 copy-start.3
  0.0 0.7 copy-done.3
  0.7 0.0 copy-start
  0.7 1.0 copy-done
  1.7 0.0 copy-start.1
  1.7 0.7 copy-done.1
  2.4 0.0 copy-start.2
  2.4 0.7 copy-done.2
  3.1 100.9 %parareal.1 = f32[1,16,32,256]{3,2,1,0:T(8,128)S(1)} custom-call(f32[16,32,256]{2,1,0:T(8,128)S(1)} %copy-done, s32[4,8,64]{2,1,0:T(8,128)S(1)} %copy-done.1, f32[1,6]{1,0:T(1,128)S(1)} %bitcast.1, f32[8,6]{1,0:T(8,128)S(1)} %copy-done.2), custom_call_target="tpu_custom_call" | custom-call | tf_op jit(solution)/shard_map/parareal/pallas_call | solution.py:484
  104.0 0.8 copy.6
Async XLA Ops:
  0.0 0.7 copy-start.3
  0.7 1.0 copy-start
  1.7 0.7 copy-start.1
  2.4 0.7 copy-start.2

commit v4 on v2

--- a/solution.py
+++ b/solution.py
@@ -13,6 +13,7 @@
 W1 = FINE_STEPS * SWEEPS
 W2 = SWEEPS
 F32 = jnp.float32
+BF16 = jnp.bfloat16
 MESH = pl.DeviceIdType.MESH
 HI = lax.Precision.HIGHEST
 
@@ -41,8 +42,9 @@
     has_prev, has_next = n > 0, n < n_count - 1
     has_lo, has_hi = s > 0, s < s_count - 1
 
-    fetches = [pltpu.make_async_copy(a, b, in_sem.at[i]) for i, (a, b) in enumerate(
-        ((init_hbm, raw), (labels_hbm, labels), (rates_hbm, rates), (heat_hbm, heat)))]
+    pairs = [(labels_hbm, labels), (rates_hbm, rates), (heat_hbm, heat)]
+    pairs += [(init_hbm.at[:, :, pl.ds(c * lanes, lanes)], raw.at[c]) for c in range(zs)]
+    fetches = [pltpu.make_async_copy(a, b, in_sem.at[i]) for i, (a, b) in enumerate(pairs)]
     for fetch in fetches:
         fetch.start()
 
@@ -197,19 +199,29 @@
 
     zi = lax.broadcasted_iota(jnp.int32, (nz, nz), 0)
     zj = lax.broadcasted_iota(jnp.int32, (nz, nz), 1)
-    to_tiles = jnp.where(zi == zs * (zj % lanes) + zj // lanes, F32(1.0), F32(0.0))
-
-    yi = lax.broadcasted_iota(jnp.int32, (ny, ny), 0)
-    yj = lax.broadcasted_iota(jnp.int32, (ny, ny), 1)
-    rows_to_tiles = jnp.where(yj == ts * (yi % cy) + yi // cy, F32(1.0), F32(0.0))
-
-    def load(p, _):
-        moved = dot(rows_to_tiles, dot(raw[p], to_tiles))
-        for t in range(ts):
-            for c in range(zs):
-                init[p, t * zs + c] = moved[t * cy:(t + 1) * cy, c * lanes:(c + 1) * lanes]
+    to_tiles = jnp.where(zi == zs * (zj % lanes) + zj // lanes, F32(1.0), F32(0.0)).astype(BF16)
+    from_tiles = jnp.where(zj == zs * (zi % lanes) + zi // lanes, F32(1.0), F32(0.0)).astype(BF16)
+
+    def permute(rows, one_hot):
+        high = rows.astype(BF16)
+        rest = rows - high.astype(F32)
+        middle = rest.astype(BF16)
+        low = (rest - middle.astype(F32)).astype(BF16)
+        parts = [jnp.dot(x, one_hot, preferred_element_type=F32) for x in (high, middle, low)]
+        return (parts[0] + parts[1]) + parts[2]
+
+    def load(q, _):
+        rows = jnp.concatenate([
+            jnp.concatenate([raw[c, 4 * q + r, pl.ds(t, cy, stride=ts), :] for c in range(zs)], 1)
+            for r in range(4) for t in range(ts)], 0)
+        moved = permute(rows, to_tiles)
+        for r in range(4):
+            for t in range(ts):
+                for c in range(zs):
+                    at = (r * ts + t) * cy
+                    init[4 * q + r, t * zs + c] = moved[at:at + cy, c * lanes:(c + 1) * lanes]
         return 0
-    lax.fori_loop(0, planes, load, 0, unroll=2)
+    lax.fori_loop(0, bx, load, 0)
 
     li = lax.broadcasted_iota(jnp.int32, (cz, lanes), 0)
     lj = lax.broadcasted_iota(jnp.int32, (cz, lanes), 1)
@@ -436,18 +448,23 @@
         copy.wait()
     kp[pad:pad + cx] = chain(1)
 
-    from_tiles = jnp.where(zj == zs * (zi % lanes) + zi // lanes, F32(1.0), F32(0.0))
-
-    rows_from_tiles = jnp.where(yi == ts * (yj % cy) + yj // cy, F32(1.0), F32(0.0))
-
-    def finish(p, _):
-        f = kp[pad + bx * s + p // 4]
-        w = u[1 + W1 + p]
-        rows = jnp.concatenate(
-            [jnp.concatenate([w[t * zs + c] + f for c in range(zs)], 1) for t in range(ts)], 0)
-        out[0, p] = dot(rows_from_tiles, dot(rows, from_tiles))
+    def finish(q, _):
+        f = kp[pad + bx * s + q]
+        rows = jnp.concatenate([
+            jnp.concatenate([u[1 + W1 + 4 * q + r, t * zs + c] + f for c in range(zs)], 1)
+            for r in range(4) for t in range(ts)], 0)
+        moved = permute(rows, from_tiles)
+        for r in range(4):
+            for t in range(ts):
+                for c in range(zs):
+                    at = (r * ts + t) * cy
+                    raw[c, 4 * q + r, pl.ds(t, cy, stride=ts), :] = moved[at:at + cy, c * lanes:(c + 1) * lanes]
         return 0
-    lax.fori_loop(0, planes, finish, 0, unroll=2)
+    lax.fori_loop(0, bx, finish, 0)
+    stores = [pltpu.make_async_copy(raw.at[c], out.at[0, :, :, pl.ds(c * lanes, lanes)], in_sem.at[c])
+              for c in range(zs)]
+    for store in stores:
+        store.start()
 
     @pl.when(first_slice & has_lo)
     def _():
@@ -471,6 +488,9 @@
     @pl.when(has_next & has_hi)
     def _():
         f_hi.wait_send()
+
+    for store in stores:
+        store.wait()
 
 
 def solution(mesh):
@@ -489,16 +509,15 @@
         def vm(*shape):
             return pltpu.VMEM(shape, F32)
 
-        vmem = pl.BlockSpec(memory_space=pltpu.VMEM)
         return pl.pallas_call(
             functools.partial(kernel, n_count, s_count),
             out_shape=jax.ShapeDtypeStruct((1, planes, ny, nz), F32),
             in_specs=[pl.BlockSpec(memory_space=pl.ANY)] * 4,
-            out_specs=vmem,
+            out_specs=pl.BlockSpec(memory_space=pl.ANY),
             scratch_shapes=[
-                vm(*init.shape), pltpu.VMEM(labels.shape, labels.dtype),
+                vm(nz // lanes, planes, ny, lanes), pltpu.VMEM(labels.shape, labels.dtype),
                 pltpu.SMEM((1, rates.shape[0]), F32), pltpu.SMEM(heat.shape, F32),
-                dma((4,)), vm(planes, *tile),
+                dma((3 + nz // lanes,)), vm(planes, *tile),
                 vm(2, cx + 2 * pad, cy, lanes),
                 vm(2, cx, cy, lanes),
                 vm(ext, *tile),

time: 100 us -> 88.3 us (0.88)
  Pallas kernels: 96.1 us -> 84.1 us
    pallas_call x1, Pallas kernels: 96.1 us -> 84.1 us  [on_device(): pl.pallas_call(functools.partial(kernel, n_count, s_count), out_shape=jax...]
where the time goes in v4:
time: 88.3 us; the launch traced here: 88 us
  Pallas kernels  84.1 us (95%)
  local copies, waits for them, and re-layouts  3.89 us (4%)
    pallas_call x1, Pallas kernels, on_device(): pl.pallas_call(functools.partial(kernel, n_count, s_count), out_shape=jax...  84.1 us
    unnamed x9, local copies, waits for them, and re-layouts  3.89 us

profile of v4, /device:TPU:27, one launch (start us, length us, event | category | flops | bytes accessed | tf_op | source)
XLA Modules:
  0.0 88.0 jit_solution(4343214738998801754)
XLA Ops:
  0.0 0.0 copy-start.3
  0.0 0.7 copy-done.3
  0.7 0.0 copy-start
  0.7 1.0 %copy-done = f32[16,32,256]{2,1,0:T(8,128)S(1)} copy-done((f32[16,32,256]{2,1,0:T(8,128)S(1)}, f32[16,32,256]{2,1,0:T(8,128)}, u32[]{:S(2)}) %copy-start) | copy-done | bytes 524312
  1.7 0.0 copy-start.1
  1.7 0.7 copy-done.1
  2.4 0.0 copy-start.2
  2.4 0.7 copy-done.2
  3.1 84.1 %parareal.1 = f32[1,16,32,256]{3,2,1,0:T(8,128)S(1)} custom-call(f32[16,32,256]{2,1,0:T(8,128)S(1)} %copy-done, s32[4,8,64]{2,1,0:T(8,128)S(1)} %copy-done.1, f32[1,6]{1,0:T(1,128)S(1)} %bitcast.1, f32[8,6]{1,0:T(8,128)S(1)} %copy-done.2), custom_call_target="tpu_custom_call" | custom-call | tf_op jit(solution)/shard_map/parareal/pallas_call | solution.py:512
  87.2 0.8 copy.6
Async XLA Ops:
  0.0 0.7 copy-start.3
  0.7 1.0 %copy-start = (f32[16,32,256]{2,1,0:T(8,128)S(1)}, f32[16,32,256]{2,1,0:T(8,128)}, u32[]{:S(2)}) copy-start(f32[16,32,256]{2,1,0:T(8,128)} %init_hbm.1) | copy-start | bytes 1572868
  1.7 0.7 copy-start.1
  2.4 0.7 copy-start.2

commit v5 on v4

--- a/solution.py
+++ b/solution.py
@@ -378,19 +378,6 @@
     off = W1 - W2
     span = planes + 2 * W2
 
-    @pl.when(first_slice)
-    def _():
-        def lay(p, _):
-            u[1 + off + p] = t0[off + p]
-            u[1 + W1 + planes + p] = t0[W1 + planes + p]
-            return 0
-        lax.fori_loop(0, W2, lay, 0)
-
-        def lay_own(p, _):
-            u[1 + W1 + p] = init[p]
-            return 0
-        lax.fori_loop(0, planes, lay_own, 0)
-
     @pl.when(has_prev)
     def _():
         c_copy.wait_recv()
@@ -413,35 +400,37 @@
             return 0
         lax.fori_loop(0, span // 4, lay, 0)
 
-    fine_step(off, span, SWEEPS)
-
-    m_lo = remote(u.at[pl.ds(1 + W1, W2)], mid.at[1], m_ss.at[0], m_rs.at[0], (n, s - 1))
-    m_hi = remote(u.at[pl.ds(1 + W1 + planes - W2, W2)], mid.at[0], m_ss.at[1], m_rs.at[1], (n, s + 1))
-
-    @pl.when(has_lo)
-    def _():
-        m_lo.start()
-
-    @pl.when(has_hi)
-    def _():
-        m_hi.start()
-
-    @pl.when(has_lo)
-    def _():
-        m_hi.wait_recv()
-        m_lo.wait_send()
-
-    @pl.when(has_hi)
-    def _():
-        m_lo.wait_recv()
-        m_hi.wait_send()
-
-    def lay_mid(p, _):
-        u[1 + off + p] = mid[0, p]
-        u[1 + W1 + planes + p] = mid[1, p]
-        return 0
-    lax.fori_loop(0, W2, lay_mid, 0)
-    fine_step(off, span, SWEEPS)
+    @pl.when(has_prev)
+    def _():
+        fine_step(off, span, SWEEPS)
+
+        m_lo = remote(u.at[pl.ds(1 + W1, W2)], mid.at[1], m_ss.at[0], m_rs.at[0], (n, s - 1))
+        m_hi = remote(u.at[pl.ds(1 + W1 + planes - W2, W2)], mid.at[0], m_ss.at[1], m_rs.at[1], (n, s + 1))
+
+        @pl.when(has_lo)
+        def _():
+            m_lo.start()
+
+        @pl.when(has_hi)
+        def _():
+            m_hi.start()
+
+        @pl.when(has_lo)
+        def _():
+            m_hi.wait_recv()
+            m_lo.wait_send()
+
+        @pl.when(has_hi)
+        def _():
+            m_lo.wait_recv()
+            m_hi.wait_send()
+
+        def lay_mid(p, _):
+            u[1 + off + p] = mid[0, p]
+            u[1 + W1 + planes + p] = mid[1, p]
+            return 0
+        lax.fori_loop(0, W2, lay_mid, 0)
+        fine_step(off, span, SWEEPS)
 
     g2 = coarse_part(1, lambda p: u[1 + W1 + p])
     for copy in g2:

time: 88.3 us -> 88.3 us (level)
  no operation moved by 1% of the time
where the time goes in v5:
time: 88.3 us; the launch traced here: 88 us
  Pallas kernels  84.1 us (95%)
  local copies, waits for them, and re-layouts  3.89 us (4%)
    pallas_call x1, Pallas kernels, on_device(): pl.pallas_call(functools.partial(kernel, n_count, s_count), out_shape=jax...  84.1 us
    unnamed x9, local copies, waits for them, and re-layouts  3.89 us

profile of v5, /device:TPU:27, one launch (start us, length us, event | category | flops | bytes accessed | tf_op | source)
XLA Modules:
  0.0 88.0 jit_solution(5834497210425712507)
XLA Ops:
  0.0 0.0 copy-start.3
  0.0 0.7 copy-done.3
  0.7 0.0 copy-start
  0.7 1.0 %copy-done = f32[16,32,256]{2,1,0:T(8,128)S(1)} copy-done((f32[16,32,256]{2,1,0:T(8,128)S(1)}, f32[16,32,256]{2,1,0:T(8,128)}, u32[]{:S(2)}) %copy-start) | copy-done | bytes 524312
  1.7 0.0 copy-start.1
  1.7 0.7 copy-done.1
  2.4 0.0 copy-start.2
  2.4 0.7 copy-done.2
  3.1 84.1 %parareal.1 = f32[1,16,32,256]{3,2,1,0:T(8,128)S(1)} custom-call(f32[16,32,256]{2,1,0:T(8,128)S(1)} %copy-done, s32[4,8,64]{2,1,0:T(8,128)S(1)} %copy-done.1, f32[1,6]{1,0:T(1,128)S(1)} %bitcast.1, f32[8,6]{1,0:T(8,128)S(1)} %copy-done.2), custom_call_target="tpu_custom_call" | custom-call | tf_op jit(solution)/shard_map/parareal/pallas_call | solution.py:501
  87.2 0.8 copy.6
Async XLA Ops:
  0.0 0.7 copy-start.3
  0.7 1.0 %copy-start = (f32[16,32,256]{2,1,0:T(8,128)S(1)}, f32[16,32,256]{2,1,0:T(8,128)}, u32[]{:S(2)}) copy-start(f32[16,32,256]{2,1,0:T(8,128)} %init_hbm.1) | copy-start | bytes 1572868
  1.7 0.7 copy-start.1
  2.4 0.7 copy-start.2
